TPU v7x, 256 devices: a whole 4x4x8 slice. The times are simulated.
256 devices in a mesh: param: 16 (over x, y), space: 2 (over core), term: 8 (over z).
Axes of the slice: x: 4, y: 4, z: 8, core: 2. Of those that a mesh axis runs over, the one named last changes fastest.
Arguments:
- fields: float32 [128, 2, 8, 128, 128], P('param', None, None, 'space'), may hold values from -4 to 4
- library: int32 [168, 4], P('term'), may hold values from 0 to 6, as said below
- centers_x: int32 [16], replicated, may hold values from 0 to 127
- centers_y: int32 [16], replicated, may hold values from 0 to 127
- centers_t: int32 [4], replicated, may hold values from 0 to 7
- groups: int32 [168], replicated, may hold values from 0 to 23
Outputs:
- coefficients: float32 [128, 2, 168], P(('param', 'term'))
- misfit: float32 [128, 2, 168], P(('param', 'term'))
Inputs may be any that keep to these rules, and one draw needn't show every extreme that they name: `library`: each row (a, b, dx, dy) gives powers a and b of 0 to 6 and derivative orders dx and dy of 0 to 2; rows are distinct, and a = b = 0 only with dx = dy = 0.
All inputs are finite; a program needn't handle non-finite values.
Results may differ from a plain program's by a relative error of at most 0.00011.
Values sent between devices are 32-bit elements; how exact they have to be, the bound alone decides.
A program may use at most 64 MiB of HBM per device.

v0:
```python
import jax
import jax.numpy as jnp
from jax import lax
from jax.sharding import PartitionSpec as P

NX = 128
NY = 128
NT = 8
POWERS = 7
TERMS = 168
TESTS = 1024
RX = 16
RT = 4
GROUPS = 24
highest = lax.Precision.HIGHEST


def space_table(centers, first_row, row_count, extent):
    cell_index = first_row + jnp.arange(row_count, dtype=jnp.int32)
    offset = (cell_index[None, :] - centers[:, None] + extent // 2) % extent - extent // 2
    scaled = offset.astype(jnp.float32) / RX
    bump_base = 1.0 - scaled * scaled
    inside = jnp.abs(scaled) < 1.0
    cube = bump_base * bump_base * bump_base
    bump_value = jnp.where(inside, cube * bump_base, 0.0)
    bump_first = jnp.where(inside, 8.0 * scaled * cube / RX, 0.0)
    bump_second = jnp.where(
        inside, -8.0 * (cube - 6.0 * scaled * scaled * bump_base * bump_base) / (RX * RX), 0.0
    )
    return jnp.stack([bump_value, bump_first, bump_second])


def time_table(centers):
    step_index = jnp.arange(NT, dtype=jnp.int32)
    scaled = (step_index[None, :] - centers[:, None]).astype(jnp.float32) / RT
    bump_base = 1.0 - scaled * scaled
    inside = jnp.abs(scaled) < 1.0
    time_bump = jnp.where(inside, bump_base * bump_base, 0.0)
    time_slope = jnp.where(inside, 4.0 * scaled * bump_base / RT, 0.0)
    return (time_bump, time_slope)


def normalize(gram_matrix):
    diagonal = jnp.diagonal(gram_matrix, axis1=1, axis2=2)
    row_scale = jnp.sqrt(diagonal / TESTS + 1e-06)
    term_scale = row_scale[:, :TERMS]
    correlation = gram_matrix[:, :TERMS, :TERMS] / (
        TESTS * term_scale[:, :, None] * term_scale[:, None, :]
    )
    right_side = gram_matrix[:, TERMS:, :TERMS] / (
        TESTS * term_scale[:, None, :] * row_scale[:, TERMS:, None]
    )
    frobenius = jnp.sqrt(jnp.sum(correlation * correlation, axis=(1, 2)))
    return (correlation, right_side, frobenius)


def group_squares(values, onehot):
    return jnp.dot(jnp.sum(values * values, axis=(0, 1)), onehot, precision=highest)


def shrink(values, totals, onehot):
    threshold = 0.7 * jnp.sqrt(jnp.mean(totals))
    per_term = jnp.dot(onehot, totals, precision=highest)
    factor = jnp.maximum(0.0, 1.0 - threshold / jnp.sqrt(per_term + 1e-12))
    return values * factor


def correlate(correlation, values):
    return jnp.einsum("pij,psj->psi", correlation, values, precision=highest)


def body(fields, library, centers_x, centers_y, centers_t, groups):
    pgroup = fields.shape[0]
    tile_rows = fields.shape[3]
    space_count = lax.axis_size("space")
    term_count = lax.axis_size("term")
    local_terms = library.shape[0]
    row_count = local_terms + 2
    half_tests = TESTS // space_count
    y_table = space_table(centers_y, 0, NY, NY)
    time_bump, time_slope = time_table(centers_t)
    x_table = space_table(centers_x, lax.axis_index("space") * tile_rows, tile_rows, NX)
    share_rows = tile_rows // term_count
    share_start = lax.axis_index("term") * share_rows
    x_share = lax.dynamic_slice_in_dim(x_table[0], share_start, share_rows, 1)
    power_a = library[:, 0]
    power_b = library[:, 1]
    orders = jnp.arange(3, dtype=jnp.int32)
    pick_x = (library[:, 2][:, None] == orders[None, :]).astype(jnp.float32)
    pick_y = (library[:, 3][:, None] == orders[None, :]).astype(jnp.float32)
    x_pick = jnp.einsum("jd,dlx->jlx", pick_x, x_table, precision=highest)
    y_pick = jnp.einsum("jd,dky->jky", pick_y, y_table, precision=highest)

    def tile_integrals(field_pair):
        species_u = field_pair[0]
        species_v = field_pair[1]
        power_u = jnp.ones((local_terms,) + species_u.shape, jnp.float32)
        power_v = jnp.ones((local_terms,) + species_v.shape, jnp.float32)
        for degree in range(1, POWERS):
            power_u = power_u * jnp.where(
                power_a[:, None, None, None] >= degree, species_u[None], 1.0
            )
            power_v = power_v * jnp.where(
                power_b[:, None, None, None] >= degree, species_v[None], 1.0
            )
        monomial = power_u * power_v
        across_y = jnp.einsum("jtxy,jky->jtxk", monomial, y_pick, precision=highest)
        across_t = jnp.einsum("jtxk,rt->jrxk", across_y, time_bump, precision=highest)
        features = jnp.einsum("jrxk,jlx->jrkl", across_t, x_pick, precision=highest).reshape(
            local_terms, TESTS
        )
        share = lax.dynamic_slice_in_dim(field_pair, share_start, share_rows, 2)
        target_y = jnp.einsum("stxy,ky->stxk", share, y_table[0], precision=highest)
        targets = jnp.einsum(
            "stxk,rt,lx->srkl", target_y, time_slope, x_share, precision=highest
        ).reshape(2, TESTS)
        joined = jnp.concatenate([features, targets], axis=0).reshape(
            row_count, space_count, half_tests
        )
        return jnp.swapaxes(joined, 0, 1)

    def fill_param(index, buffer):
        field_pair = lax.dynamic_index_in_dim(fields, index, 0, keepdims=False)
        return lax.dynamic_update_slice_in_dim(
            buffer, tile_integrals(field_pair)[:, None], index, 1
        )

    buffer = jnp.zeros((space_count, pgroup, row_count, half_tests), jnp.float32)
    buffer = lax.fori_loop(0, pgroup, fill_param, buffer)
    received = lax.all_to_all(
        buffer.reshape(space_count * pgroup, row_count, half_tests),
        ("space", "term"),
        split_axis=0,
        concat_axis=1,
        tiled=True,
    )
    blocks = jnp.sum(received.reshape(space_count, term_count, row_count, half_tests), axis=0)
    features_half = blocks[:, :local_terms].reshape(term_count * local_terms, half_tests)
    targets_half = jnp.sum(blocks[:, local_terms:], axis=0)
    half_rows = jnp.concatenate([features_half, targets_half], axis=0)
    whole_rows = lax.all_gather(half_rows, "space", axis=1, tiled=True)
    gram_matrix = jnp.dot(whole_rows, whole_rows.T, precision=highest)[None]
    correlation, right_side, frobenius = normalize(gram_matrix)
    onehot = (groups[:, None] == jnp.arange(GROUPS, dtype=jnp.int32)[None, :]).astype(jnp.float32)
    largest = lax.pmax(jnp.max(frobenius), ("param", "term"))
    step_size = 1.0 / largest
    first_guess = step_size * right_side
    first_sq = lax.psum(group_squares(first_guess, onehot), ("param", "term"))
    first = shrink(first_guess, first_sq, onehot)
    second_guess = first - step_size * (correlate(correlation, first) - right_side)
    second_sq = lax.psum(group_squares(second_guess, onehot), ("param", "term"))
    second = shrink(second_guess, second_sq, onehot)
    coefficients = second / step_size
    misfit = right_side - correlate(correlation, second)
    return (coefficients, misfit)


def solution(mesh):
    return jax.shard_map(
        body,
        mesh=mesh,
        in_specs=(P("param", None, None, "space", None), P("term", None), P(), P(), P(), P()),
        out_specs=(P(("param", "term"), None, None), P(("param", "term"), None, None)),
        check_vma=False,
    )
```

profile of v0, /device:TPU:0, one launch (start us, length us, event | category | flops | bytes accessed | tf_op | source)
XLA Modules:
  0.0 1257.9 jit_solution(2309411352389409611)
XLA Ops:
  0.6 0.8 multiply_select_fusion.2
  1.5 0.7 fusion.127
  2.2 0.8 slice_bitcast_fusion.1
  3.4 0.8 multiply_select_fusion.5
  4.6 175.0 %while.18 = (s32[]{:T(128)}, f32[2,8,23,512]{3,0,2,1:T(2,128)S(1)}, s32[21,1]{0,1:T(1,128)S(1)}, f32[8,2,8,64,128]{4,3,2,1,0:T(8,128)}, s32[21,1]{0,1:T(1,128)S(...) while((s32[]{:T(128)}, f32[2,8,23,512]{3,0,2,1:T(2,128)S(1)}, ...), condition=%wide.region_1.2_spmd.clone.clone, body=%wide.region_0.1_spmd.clone.clone.sunk | while | flops 324181856 | bytes 4605749 | solution.py:129
  4.6 1.1 dynamic-slice_bitcast_fusion.6
  5.7 16.0 %fusion.203 = f32[21,8,64,16]{2,3,1,0:T(8,128)S(1)} fusion(f32[8,64,128]{2,1,0:T(8,128)S(1)} %get-tuple-element.566, f32[8,64,128]{2,1,0:T(8,128)S(1)} %get-tuple-element.567, pred[21]{0:T(512)(128)(4,1)S(1)} %get-tuple-element.568, pred[21]{0:T(512)(128)(4,1)S(1)} %get-tuple-element.569, pred[21]{0:T(512)(128)(4,1)S(1)} %get-tuple-element.570, ...), kind=kOutput, calls=%fused_computation.4.clone.1 | convolution fusion | flops 295895040 | bytes 1384700 | tf_op jit(solution)/shard_map/while/body/eval_jaxpr/jtxy,jky->jtxk/dot_general | solution.py:107
  21.7 1.6 fusion.204
  23.4 0.7 fusion.205
  24.1 0.4 concatenate.36
  24.5 0.9 dynamic-slice_bitcast_fusion.5
  26.5 1.1 dynamic-slice_bitcast_fusion.6
  27.6 16.0 %fusion.203 = f32[21,8,64,16]{2,3,1,0:T(8,128)S(1)} fusion(f32[8,64,128]{2,1,0:T(8,128)S(1)} %get-tuple-element.566, f32[8,64,128]{2,1,0:T(8,128)S(1)} %get-tuple-element.567, pred[21]{0:T(512)(128)(4,1)S(1)} %get-tuple-element.568, pred[21]{0:T(512)(128)(4,1)S(1)} %get-tuple-element.569, pred[21]{0:T(512)(128)(4,1)S(1)} %get-tuple-element.570, ...), kind=kOutput, calls=%fused_computation.4.clone.1 | convolution fusion | flops 295895040 | bytes 1384700 | tf_op jit(solution)/shard_map/while/body/eval_jaxpr/jtxy,jky->jtxk/dot_general | solution.py:107
  43.6 1.6 fusion.204
  45.2 0.7 fusion.205
  46.3 0.9 dynamic-slice_bitcast_fusion.5
  48.3 1.1 dynamic-slice_bitcast_fusion.6
  49.4 16.0 %fusion.203 = f32[21,8,64,16]{2,3,1,0:T(8,128)S(1)} fusion(f32[8,64,128]{2,1,0:T(8,128)S(1)} %get-tuple-element.566, f32[8,64,128]{2,1,0:T(8,128)S(1)} %get-tuple-element.567, pred[21]{0:T(512)(128)(4,1)S(1)} %get-tuple-element.568, pred[21]{0:T(512)(128)(4,1)S(1)} %get-tuple-element.569, pred[21]{0:T(512)(128)(4,1)S(1)} %get-tuple-element.570, ...), kind=kOutput, calls=%fused_computation.4.clone.1 | convolution fusion | flops 295895040 | bytes 1384700 | tf_op jit(solution)/shard_map/while/body/eval_jaxpr/jtxy,jky->jtxk/dot_general | solution.py:107
  65.4 1.6 fusion.204
  67.1 0.7 fusion.205
  67.8 0.4 concatenate.36
  68.2 0.9 dynamic-slice_bitcast_fusion.5
  70.2 1.1 dynamic-slice_bitcast_fusion.6
  71.3 16.0 %fusion.203 = f32[21,8,64,16]{2,3,1,0:T(8,128)S(1)} fusion(f32[8,64,128]{2,1,0:T(8,128)S(1)} %get-tuple-element.566, f32[8,64,128]{2,1,0:T(8,128)S(1)} %get-tuple-element.567, pred[21]{0:T(512)(128)(4,1)S(1)} %get-tuple-element.568, pred[21]{0:T(512)(128)(4,1)S(1)} %get-tuple-element.569, pred[21]{0:T(512)(128)(4,1)S(1)} %get-tuple-element.570, ...), kind=kOutput, calls=%fused_computation.4.clone.1 | convolution fusion | flops 295895040 | bytes 1384700 | tf_op jit(solution)/shard_map/while/body/eval_jaxpr/jtxy,jky->jtxk/dot_general | solution.py:107
  87.3 1.6 fusion.204
  88.9 0.7 fusion.205
  89.6 0.4 concatenate.36
  90.0 0.9 dynamic-slice_bitcast_fusion.5
  92.1 1.1 dynamic-slice_bitcast_fusion.6
  93.1 16.0 %fusion.203 = f32[21,8,64,16]{2,3,1,0:T(8,128)S(1)} fusion(f32[8,64,128]{2,1,0:T(8,128)S(1)} %get-tuple-element.566, f32[8,64,128]{2,1,0:T(8,128)S(1)} %get-tuple-element.567, pred[21]{0:T(512)(128)(4,1)S(1)} %get-tuple-element.568, pred[21]{0:T(512)(128)(4,1)S(1)} %get-tuple-element.569, pred[21]{0:T(512)(128)(4,1)S(1)} %get-tuple-element.570, ...), kind=kOutput, calls=%fused_computation.4.clone.1 | convolution fusion | flops 295895040 | bytes 1384700 | tf_op jit(solution)/shard_map/while/body/eval_jaxpr/jtxy,jky->jtxk/dot_general | solution.py:107
  109.1 1.6 fusion.204
  110.8 0.7 fusion.205
  111.5 0.4 concatenate.36
  111.9 0.9 dynamic-slice_bitcast_fusion.5
  113.9 1.1 dynamic-slice_bitcast_fusion.6
  115.0 16.0 %fusion.203 = f32[21,8,64,16]{2,3,1,0:T(8,128)S(1)} fusion(f32[8,64,128]{2,1,0:T(8,128)S(1)} %get-tuple-element.566, f32[8,64,128]{2,1,0:T(8,128)S(1)} %get-tuple-element.567, pred[21]{0:T(512)(128)(4,1)S(1)} %get-tuple-element.568, pred[21]{0:T(512)(128)(4,1)S(1)} %get-tuple-element.569, pred[21]{0:T(512)(128)(4,1)S(1)} %get-tuple-element.570, ...), kind=kOutput, calls=%fused_computation.4.clone.1 | convolution fusion | flops 295895040 | bytes 1384700 | tf_op jit(solution)/shard_map/while/body/eval_jaxpr/jtxy,jky->jtxk/dot_general | solution.py:107
  131.0 1.6 fusion.204
  132.6 0.7 fusion.205
  133.7 0.9 dynamic-slice_bitcast_fusion.5
  135.8 1.1 dynamic-slice_bitcast_fusion.6
  136.9 16.0 %fusion.203 = f32[21,8,64,16]{2,3,1,0:T(8,128)S(1)} fusion(f32[8,64,128]{2,1,0:T(8,128)S(1)} %get-tuple-element.566, f32[8,64,128]{2,1,0:T(8,128)S(1)} %get-tuple-element.567, pred[21]{0:T(512)(128)(4,1)S(1)} %get-tuple-element.568, pred[21]{0:T(512)(128)(4,1)S(1)} %get-tuple-element.569, pred[21]{0:T(512)(128)(4,1)S(1)} %get-tuple-element.570, ...), kind=kOutput, calls=%fused_computation.4.clone.1 | convolution fusion | flops 295895040 | bytes 1384700 | tf_op jit(solution)/shard_map/while/body/eval_jaxpr/jtxy,jky->jtxk/dot_general | solution.py:107
  152.8 1.6 fusion.204
  154.5 0.7 fusion.205
  155.6 0.9 dynamic-slice_bitcast_fusion.5
  157.6 1.1 dynamic-slice_bitcast_fusion.6
  158.7 16.0 %fusion.203 = f32[21,8,64,16]{2,3,1,0:T(8,128)S(1)} fusion(f32[8,64,128]{2,1,0:T(8,128)S(1)} %get-tuple-element.566, f32[8,64,128]{2,1,0:T(8,128)S(1)} %get-tuple-element.567, pred[21]{0:T(512)(128)(4,1)S(1)} %get-tuple-element.568, pred[21]{0:T(512)(128)(4,1)S(1)} %get-tuple-element.569, pred[21]{0:T(512)(128)(4,1)S(1)} %get-tuple-element.570, ...), kind=kOutput, calls=%fused_computation.4.clone.1 | convolution fusion | flops 295895040 | bytes 1384700 | tf_op jit(solution)/shard_map/while/body/eval_jaxpr/jtxy,jky->jtxk/dot_general | solution.py:107
  174.7 1.6 fusion.204
  176.3 0.7 fusion.205
  177.1 0.4 concatenate.36
  177.5 0.9 dynamic-slice_bitcast_fusion.5
  179.6 1.0 copy.33
  180.7 7.0 all-to-all-start
  187.6 20.5 %all-to-all-done = f32[16,23,512]{2,1,0:T(8,128)S(1)} async-done(((f32[16,23,512]{2,1,0:T(8,128)}), f32[16,23,512]{2,1,0:T(8,128)S(1)}, u32[]{:S(2)}, u32[]{:S(2)}) %all-to-all-start) | async-done | bytes 753696 | tf_op jit(solution)/shard_map/all_to_all | solution.py:130
  208.4 3.0 all_gather.3
  211.4 0.7 fusion.167
  212.2 2.8 gather_fusion
  215.0 0.7 multiply_reduce_fusion
  216.5 349.0 %pmax.7 = f32[]{:T(128)} all-reduce(f32[]{:T(128)S(6)} %sqrt.28), channel_id=1, replica_groups=mesh['param'=16,'space'=2,'term'=8] {'param','term'}, use_global_device_ids=true, to_apply=%region_5.6 | all-reduce | flops 1 | bytes 8 | tf_op jit(solution)/shard_map/pmax | solution.py:145
  566.5 342.2 %psum.14 = f32[24]{0:T(128)S(1)} all-reduce(f32[24]{0:T(128)S(1)} %convolution_bitcast_fusion.5), channel_id=1, replica_groups=mesh['param'=16,'space'=2,'term'=8] {'param','term'}, use_global_device_ids=true, to_apply=%region_7.8 | all-reduce | flops 24 | bytes 192 | tf_op jit(solution)/shard_map/psum | solution.py:148
  908.7 0.6 reduce_sum.67
  910.7 344.2 %psum.15 = f32[24]{0:T(128)S(1)} all-reduce(f32[24]{0:T(128)S(1)} %convolution_bitcast_fusion.4), channel_id=1, replica_groups=mesh['param'=16,'space'=2,'term'=8] {'param','term'}, use_global_device_ids=true, to_apply=%region_10.11 | all-reduce | flops 24 | bytes 192 | tf_op jit(solution)/shard_map/psum | solution.py:151
  1254.9 0.6 reduce_sum.69
  1256.5 0.8 fusion.112
  1257.4 0.6 multiply_divide_fusion
  (116 shorter events, 11.5 us)
Async XLA Ops:
  5.7 16.0 %copy-start = (s32[4]{0:T(128)S(1)}, s32[4]{0:T(128)}, u32[]{:S(2)}) copy-start(s32[4]{0:T(128)} %get-tuple-element.619) | copy-start | bytes 52 | tf_op jit(solution)/shard_map/while
  21.7 3.7 copy-start.1
  27.6 16.0 %copy-start = (s32[4]{0:T(128)S(1)}, s32[4]{0:T(128)}, u32[]{:S(2)}) copy-start(s32[4]{0:T(128)} %get-tuple-element.619) | copy-start | bytes 52 | tf_op jit(solution)/shard_map/while
  43.5 3.7 copy-start.1
  49.4 16.0 %copy-start = (s32[4]{0:T(128)S(1)}, s32[4]{0:T(128)}, u32[]{:S(2)}) copy-start(s32[4]{0:T(128)} %get-tuple-element.619) | copy-start | bytes 52 | tf_op jit(solution)/shard_map/while
  65.4 3.7 copy-start.1
  71.3 16.0 %copy-start = (s32[4]{0:T(128)S(1)}, s32[4]{0:T(128)}, u32[]{:S(2)}) copy-start(s32[4]{0:T(128)} %get-tuple-element.619) | copy-start | bytes 52 | tf_op jit(solution)/shard_map/while
  87.2 3.7 copy-start.1
  93.1 16.0 %copy-start = (s32[4]{0:T(128)S(1)}, s32[4]{0:T(128)}, u32[]{:S(2)}) copy-start(s32[4]{0:T(128)} %get-tuple-element.619) | copy-start | bytes 52 | tf_op jit(solution)/shard_map/while
  109.1 3.7 copy-start.1
  115.0 16.0 %copy-start = (s32[4]{0:T(128)S(1)}, s32[4]{0:T(128)}, u32[]{:S(2)}) copy-start(s32[4]{0:T(128)} %get-tuple-element.619) | copy-start | bytes 52 | tf_op jit(solution)/shard_map/while
  131.0 3.7 copy-start.1
  136.8 16.0 %copy-start = (s32[4]{0:T(128)S(1)}, s32[4]{0:T(128)}, u32[]{:S(2)}) copy-start(s32[4]{0:T(128)} %get-tuple-element.619) | copy-start | bytes 52 | tf_op jit(solution)/shard_map/while
  152.8 3.7 copy-start.1
  158.7 16.0 %copy-start = (s32[4]{0:T(128)S(1)}, s32[4]{0:T(128)}, u32[]{:S(2)}) copy-start(s32[4]{0:T(128)} %get-tuple-element.619) | copy-start | bytes 52 | tf_op jit(solution)/shard_map/while
  174.7 3.7 copy-start.1
  180.7 385.7 %copy-start.2 = (s32[168]{0:T(256)S(1)}, s32[168]{0:T(256)}, u32[]{:S(2)}) copy-start(s32[168]{0:T(256)} %param.13) | copy-start | bytes 2020
  180.7 27.5 %all-to-all-start = ((f32[16,23,512]{2,1,0:T(8,128)}), f32[16,23,512]{2,1,0:T(8,128)S(1)}, u32[]{:S(2)}, u32[]{:S(2)}) async-start(f32[16,23,512]{2,1,0:T(8,128)} %bitcast.5), calls=%async_computation | async-start | bytes 1572864 | tf_op jit(solution)/shard_map/all_to_all | solution.py:130
where the time goes:
time: 1260 us
  blocking collectives  1040 us (83%)
  matrix products  157 us (12%)
  local copies, waits for them, and re-layouts  24.8 us (2%)
  waiting for transfers between devices  20.5 us (2%)
    pmax x1, blocking collectives, body(): largest = lax.pmax(jnp.max(frobenius), ('param', 'term'))  349 us
    psum x1, blocking collectives, body(): second_sq = lax.psum(group_squares(second_guess, onehot), ('param', 'term'))  344 us
    psum x1, blocking collectives, body(): first_sq = lax.psum(group_squares(first_guess, onehot), ('param', 'term'))  342 us
    dot_general x8, matrix products, tile_integrals(): across_y = jnp.einsum('jtxy,jky->jtxk', monomial, y_pick, precision=highest)  128 us
  transfers between devices with their start and end apart: 1, of which 1 were waited for; matrix products, arithmetic and copies ran while one was open for 0% of the time, Pallas kernels for 0%

commit v1 on v0

--- a/solution.py
+++ b/solution.py
@@ -148,7 +148,9 @@
     first_sq = lax.psum(group_squares(first_guess, onehot), ("param", "term"))
     first = shrink(first_guess, first_sq, onehot)
     second_guess = first - step_size * (correlate(correlation, first) - right_side)
-    second_sq = lax.psum(group_squares(second_guess, onehot), ("param", "term"))
+    second_sq = group_squares(second_guess, onehot)
+    for over in ("param", "term"):
+        second_sq = lax.psum(second_sq, over)
     second = shrink(second_guess, second_sq, onehot)
     coefficients = second / step_size
     misfit = right_side - correlate(correlation, second)

time: 1260 us -> 968 us (0.77)
  blocking collectives: 1040 us -> 746 us
    psum x1 -> x2, blocking collectives: 344 us -> 52.2 us  [body(): second_sq = lax.psum(second_sq, over)]
where the time goes in v1:
time: 968 us; the launch traced here: 966 us
  blocking collectives  746 us (77%)
  matrix products  157 us (16%)
  local copies, waits for them, and re-layouts  24.8 us (3%)
  waiting for transfers between devices  20.5 us (2%)
    pmax x1, blocking collectives, body(): largest = lax.pmax(jnp.max(frobenius), ('param', 'term'))  349 us
    psum x1, blocking collectives, body(): first_sq = lax.psum(group_squares(first_guess, onehot), ('param', 'term'))  342 us
    dot_general x8, matrix products, tile_integrals(): across_y = jnp.einsum('jtxy,jky->jtxk', monomial, y_pick, precision=highest)  128 us
    psum x2, blocking collectives, body(): second_sq = lax.psum(second_sq, over)  52.2 us
    all_to_all x1, waiting for transfers between devices, body(): lax.all_to_all(buffer.reshape(space_count * pgroup, row_count, half_tests...  20.5 us
  transfers between devices with their start and end apart: 1, of which 1 were waited for; matrix products, arithmetic and copies ran while one was open for 0% of the time, Pallas kernels for 0%

profile of v1, /device:TPU:0, one launch (start us, length us, event | category | flops | bytes accessed | tf_op | source)
XLA Modules:
  0.0 965.9 jit_solution(1410907970549381623)
XLA Ops:
  0.6 0.8 multiply_select_fusion.2
  1.5 0.7 fusion.127
  2.2 0.8 slice_bitcast_fusion.1
  3.4 0.8 multiply_select_fusion.5
  4.6 175.0 %while.18 = (s32[]{:T(128)}, f32[2,8,23,512]{3,0,2,1:T(2,128)S(1)}, s32[21,1]{0,1:T(1,128)S(1)}, f32[8,2,8,64,128]{4,3,2,1,0:T(8,128)}, s32[21,1]{0,1:T(1,128)S(...) while((s32[]{:T(128)}, f32[2,8,23,512]{3,0,2,1:T(2,128)S(1)}, ...), condition=%wide.region_1.2_spmd.clone.clone, body=%wide.region_0.1_spmd.clone.clone.sunk | while | flops 324181856 | bytes 4605749 | solution.py:129
  4.6 1.1 dynamic-slice_bitcast_fusion.6
  5.7 16.0 %fusion.203 = f32[21,8,64,16]{2,3,1,0:T(8,128)S(1)} fusion(f32[8,64,128]{2,1,0:T(8,128)S(1)} %get-tuple-element.566, f32[8,64,128]{2,1,0:T(8,128)S(1)} %get-tuple-element.567, pred[21]{0:T(512)(128)(4,1)S(1)} %get-tuple-element.568, pred[21]{0:T(512)(128)(4,1)S(1)} %get-tuple-element.569, pred[21]{0:T(512)(128)(4,1)S(1)} %get-tuple-element.570, ...), kind=kOutput, calls=%fused_computation.4.clone.1 | convolution fusion | flops 295895040 | bytes 1384700 | tf_op jit(solution)/shard_map/while/body/eval_jaxpr/jtxy,jky->jtxk/dot_general | solution.py:107
  21.7 1.6 fusion.204
  23.4 0.7 fusion.205
  24.1 0.4 concatenate.36
  24.5 0.9 dynamic-slice_bitcast_fusion.5
  26.5 1.1 dynamic-slice_bitcast_fusion.6
  27.6 16.0 %fusion.203 = f32[21,8,64,16]{2,3,1,0:T(8,128)S(1)} fusion(f32[8,64,128]{2,1,0:T(8,128)S(1)} %get-tuple-element.566, f32[8,64,128]{2,1,0:T(8,128)S(1)} %get-tuple-element.567, pred[21]{0:T(512)(128)(4,1)S(1)} %get-tuple-element.568, pred[21]{0:T(512)(128)(4,1)S(1)} %get-tuple-element.569, pred[21]{0:T(512)(128)(4,1)S(1)} %get-tuple-element.570, ...), kind=kOutput, calls=%fused_computation.4.clone.1 | convolution fusion | flops 295895040 | bytes 1384700 | tf_op jit(solution)/shard_map/while/body/eval_jaxpr/jtxy,jky->jtxk/dot_general | solution.py:107
  43.6 1.6 fusion.204
  45.2 0.7 fusion.205
  46.3 0.9 dynamic-slice_bitcast_fusion.5
  48.3 1.1 dynamic-slice_bitcast_fusion.6
  49.4 16.0 %fusion.203 = f32[21,8,64,16]{2,3,1,0:T(8,128)S(1)} fusion(f32[8,64,128]{2,1,0:T(8,128)S(1)} %get-tuple-element.566, f32[8,64,128]{2,1,0:T(8,128)S(1)} %get-tuple-element.567, pred[21]{0:T(512)(128)(4,1)S(1)} %get-tuple-element.568, pred[21]{0:T(512)(128)(4,1)S(1)} %get-tuple-element.569, pred[21]{0:T(512)(128)(4,1)S(1)} %get-tuple-element.570, ...), kind=kOutput, calls=%fused_computation.4.clone.1 | convolution fusion | flops 295895040 | bytes 1384700 | tf_op jit(solution)/shard_map/while/body/eval_jaxpr/jtxy,jky->jtxk/dot_general | solution.py:107
  65.4 1.6 fusion.204
  67.1 0.7 fusion.205
  67.8 0.4 concatenate.36
  68.2 0.9 dynamic-slice_bitcast_fusion.5
  70.2 1.1 dynamic-slice_bitcast_fusion.6
  71.3 16.0 %fusion.203 = f32[21,8,64,16]{2,3,1,0:T(8,128)S(1)} fusion(f32[8,64,128]{2,1,0:T(8,128)S(1)} %get-tuple-element.566, f32[8,64,128]{2,1,0:T(8,128)S(1)} %get-tuple-element.567, pred[21]{0:T(512)(128)(4,1)S(1)} %get-tuple-element.568, pred[21]{0:T(512)(128)(4,1)S(1)} %get-tuple-element.569, pred[21]{0:T(512)(128)(4,1)S(1)} %get-tuple-element.570, ...), kind=kOutput, calls=%fused_computation.4.clone.1 | convolution fusion | flops 295895040 | bytes 1384700 | tf_op jit(solution)/shard_map/while/body/eval_jaxpr/jtxy,jky->jtxk/dot_general | solution.py:107
  87.3 1.6 fusion.204
  88.9 0.7 fusion.205
  89.6 0.4 concatenate.36
  90.0 0.9 dynamic-slice_bitcast_fusion.5
  92.1 1.1 dynamic-slice_bitcast_fusion.6
  93.1 16.0 %fusion.203 = f32[21,8,64,16]{2,3,1,0:T(8,128)S(1)} fusion(f32[8,64,128]{2,1,0:T(8,128)S(1)} %get-tuple-element.566, f32[8,64,128]{2,1,0:T(8,128)S(1)} %get-tuple-element.567, pred[21]{0:T(512)(128)(4,1)S(1)} %get-tuple-element.568, pred[21]{0:T(512)(128)(4,1)S(1)} %get-tuple-element.569, pred[21]{0:T(512)(128)(4,1)S(1)} %get-tuple-element.570, ...), kind=kOutput, calls=%fused_computation.4.clone.1 | convolution fusion | flops 295895040 | bytes 1384700 | tf_op jit(solution)/shard_map/while/body/eval_jaxpr/jtxy,jky->jtxk/dot_general | solution.py:107
  109.1 1.6 fusion.204
  110.8 0.7 fusion.205
  111.5 0.4 concatenate.36
  111.9 0.9 dynamic-slice_bitcast_fusion.5
  113.9 1.1 dynamic-slice_bitcast_fusion.6
  115.0 16.0 %fusion.203 = f32[21,8,64,16]{2,3,1,0:T(8,128)S(1)} fusion(f32[8,64,128]{2,1,0:T(8,128)S(1)} %get-tuple-element.566, f32[8,64,128]{2,1,0:T(8,128)S(1)} %get-tuple-element.567, pred[21]{0:T(512)(128)(4,1)S(1)} %get-tuple-element.568, pred[21]{0:T(512)(128)(4,1)S(1)} %get-tuple-element.569, pred[21]{0:T(512)(128)(4,1)S(1)} %get-tuple-element.570, ...), kind=kOutput, calls=%fused_computation.4.clone.1 | convolution fusion | flops 295895040 | bytes 1384700 | tf_op jit(solution)/shard_map/while/body/eval_jaxpr/jtxy,jky->jtxk/dot_general | solution.py:107
  131.0 1.6 fusion.204
  132.6 0.7 fusion.205
  133.7 0.9 dynamic-slice_bitcast_fusion.5
  135.8 1.1 dynamic-slice_bitcast_fusion.6
  136.9 16.0 %fusion.203 = f32[21,8,64,16]{2,3,1,0:T(8,128)S(1)} fusion(f32[8,64,128]{2,1,0:T(8,128)S(1)} %get-tuple-element.566, f32[8,64,128]{2,1,0:T(8,128)S(1)} %get-tuple-element.567, pred[21]{0:T(512)(128)(4,1)S(1)} %get-tuple-element.568, pred[21]{0:T(512)(128)(4,1)S(1)} %get-tuple-element.569, pred[21]{0:T(512)(128)(4,1)S(1)} %get-tuple-element.570, ...), kind=kOutput, calls=%fused_computation.4.clone.1 | convolution fusion | flops 295895040 | bytes 1384700 | tf_op jit(solution)/shard_map/while/body/eval_jaxpr/jtxy,jky->jtxk/dot_general | solution.py:107
  152.8 1.6 fusion.204
  154.5 0.7 fusion.205
  155.6 0.9 dynamic-slice_bitcast_fusion.5
  157.6 1.1 dynamic-slice_bitcast_fusion.6
  158.7 16.0 %fusion.203 = f32[21,8,64,16]{2,3,1,0:T(8,128)S(1)} fusion(f32[8,64,128]{2,1,0:T(8,128)S(1)} %get-tuple-element.566, f32[8,64,128]{2,1,0:T(8,128)S(1)} %get-tuple-element.567, pred[21]{0:T(512)(128)(4,1)S(1)} %get-tuple-element.568, pred[21]{0:T(512)(128)(4,1)S(1)} %get-tuple-element.569, pred[21]{0:T(512)(128)(4,1)S(1)} %get-tuple-element.570, ...), kind=kOutput, calls=%fused_computation.4.clone.1 | convolution fusion | flops 295895040 | bytes 1384700 | tf_op jit(solution)/shard_map/while/body/eval_jaxpr/jtxy,jky->jtxk/dot_general | solution.py:107
  174.7 1.6 fusion.204
  176.3 0.7 fusion.205
  177.5 0.9 dynamic-slice_bitcast_fusion.5
  179.6 1.0 copy.33
  180.7 7.0 all-to-all-start
  187.6 20.5 %all-to-all-done = f32[16,23,512]{2,1,0:T(8,128)S(1)} async-done(((f32[16,23,512]{2,1,0:T(8,128)}), f32[16,23,512]{2,1,0:T(8,128)S(1)}, u32[]{:S(2)}, u32[]{:S(2)}) %all-to-all-start) | async-done | bytes 753696 | tf_op jit(solution)/shard_map/all_to_all | solution.py:130
  208.4 3.0 all_gather.3
  211.4 0.7 fusion.167
  212.2 2.8 gather_fusion
  215.0 0.7 multiply_reduce_fusion
  216.5 349.0 %pmax.7 = f32[]{:T(128)} all-reduce(f32[]{:T(128)S(6)} %sqrt.28), channel_id=1, replica_groups=mesh['param'=16,'space'=2,'term'=8] {'param','term'}, use_global_device_ids=true, to_apply=%region_5.6 | all-reduce | flops 1 | bytes 8 | tf_op jit(solution)/shard_map/pmax | solution.py:145
  566.5 342.2 %psum.21 = f32[24]{0:T(128)S(1)} all-reduce(f32[24]{0:T(128)S(1)} %convolution_bitcast_fusion.5), channel_id=1, replica_groups=mesh['param'=16,'space'=2,'term'=8] {'param','term'}, use_global_device_ids=true, to_apply=%region_7.8 | all-reduce | flops 24 | bytes 192 | tf_op jit(solution)/shard_map/psum | solution.py:148
  908.7 0.6 reduce_sum.67
  910.7 35.5 %psum.22 = f32[24]{0:T(128)S(1)} all-reduce(f32[24]{0:T(128)S(1)} %convolution_bitcast_fusion.4), channel_id=1, replica_groups=mesh['param'=16,'space'=2,'term'=8] {'param'}, use_global_device_ids=true, to_apply=%region_10.11 | all-reduce | flops 24 | bytes 192 | tf_op jit(solution)/shard_map/psum | solution.py:153
  946.2 16.7 %psum.23 = f32[24]{0:T(128)S(1)} all-reduce(f32[24]{0:T(128)S(1)} %psum.22), channel_id=1, replica_groups=mesh['param'=16,'space'=2,'term'=8] {'term'}, use_global_device_ids=true, to_apply=%region_11.12 | all-reduce | flops 24 | bytes 192 | tf_op jit(solution)/shard_map/psum | solution.py:153
  962.9 0.6 reduce_sum.69
  964.5 0.8 fusion.112
  965.3 0.6 multiply_divide_fusion
  (117 shorter events, 11.9 us)
Async XLA Ops:
  5.7 16.0 %copy-start = (s32[4]{0:T(128)S(1)}, s32[4]{0:T(128)}, u32[]{:S(2)}) copy-start(s32[4]{0:T(128)} %get-tuple-element.619) | copy-start | bytes 52 | tf_op jit(solution)/shard_map/while
  21.7 3.7 copy-start.1
  27.6 16.0 %copy-start = (s32[4]{0:T(128)S(1)}, s32[4]{0:T(128)}, u32[]{:S(2)}) copy-start(s32[4]{0:T(128)} %get-tuple-element.619) | copy-start | bytes 52 | tf_op jit(solution)/shard_map/while
  43.5 3.7 copy-start.1
  49.4 16.0 %copy-start = (s32[4]{0:T(128)S(1)}, s32[4]{0:T(128)}, u32[]{:S(2)}) copy-start(s32[4]{0:T(128)} %get-tuple-element.619) | copy-start | bytes 52 | tf_op jit(solution)/shard_map/while
  65.4 3.7 copy-start.1
  71.3 16.0 %copy-start = (s32[4]{0:T(128)S(1)}, s32[4]{0:T(128)}, u32[]{:S(2)}) copy-start(s32[4]{0:T(128)} %get-tuple-element.619) | copy-start | bytes 52 | tf_op jit(solution)/shard_map/while
  87.2 3.7 copy-start.1
  93.1 16.0 %copy-start = (s32[4]{0:T(128)S(1)}, s32[4]{0:T(128)}, u32[]{:S(2)}) copy-start(s32[4]{0:T(128)} %get-tuple-element.619) | copy-start | bytes 52 | tf_op jit(solution)/shard_map/while
  109.1 3.7 copy-start.1
  115.0 16.0 %copy-start = (s32[4]{0:T(128)S(1)}, s32[4]{0:T(128)}, u32[]{:S(2)}) copy-start(s32[4]{0:T(128)} %get-tuple-element.619) | copy-start | bytes 52 | tf_op jit(solution)/shard_map/while
  131.0 3.7 copy-start.1
  136.8 16.0 %copy-start = (s32[4]{0:T(128)S(1)}, s32[4]{0:T(128)}, u32[]{:S(2)}) copy-start(s32[4]{0:T(128)} %get-tuple-element.619) | copy-start | bytes 52 | tf_op jit(solution)/shard_map/while
  152.8 3.7 copy-start.1
  158.7 16.0 %copy-start = (s32[4]{0:T(128)S(1)}, s32[4]{0:T(128)}, u32[]{:S(2)}) copy-start(s32[4]{0:T(128)} %get-tuple-element.619) | copy-start | bytes 52 | tf_op jit(solution)/shard_map/while
  174.7 3.7 copy-start.1
  180.7 385.7 %copy-start.2 = (s32[168]{0:T(256)S(1)}, s32[168]{0:T(256)}, u32[]{:S(2)}) copy-start(s32[168]{0:T(256)} %param.13) | copy-start | bytes 2020
  180.7 27.5 %all-to-all-start = ((f32[16,23,512]{2,1,0:T(8,128)}), f32[16,23,512]{2,1,0:T(8,128)S(1)}, u32[]{:S(2)}, u32[]{:S(2)}) async-start(f32[16,23,512]{2,1,0:T(8,128)} %bitcast.5), calls=%async_computation | async-start | bytes 1572864 | tf_op jit(solution)/shard_map/all_to_all | solution.py:130
